TPU v7x, 256 devices: a whole 4x4x8 slice. The times are simulated.
256 devices in a mesh: pop: 32 (over z_hi, x, core), shard: 8 (over z_lo, y).
Axes of the slice: x: 4, y: 4, z: 8 (z_hi: 4, z_lo: 2; z = z_hi * 2 + z_lo), core: 2. Of those that a mesh axis runs over, the one named last changes fastest.
Arguments:
- hidden: bfloat16 [64, 4096, 4096], P('pop', 'shard'), may hold values from -6 to 6
- norm_scale_vector: float32 [4096], replicated, may hold values from 0.3 to 3
- w_value: bfloat16 [4096, 1024], P('shard'), may hold values from -0.09375 to 0.09375
- model_side_factor: bfloat16 [64, 4, 4096], P('pop'), may hold values from -0.09375 to 0.09375
- value_side_factor: bfloat16 [64, 4, 1024], P('pop'), may hold values from -3 to 3
- target: bfloat16 [64, 4096, 1024], P('pop', 'shard'), may hold values from -6 to 6
- lengths: int32 [64], P('pop'), may hold values from 1 to 4096, 163840 in all
- fitness_ranks: int32 [64], replicated, may hold values from 0 to 63, each once
Outputs:
- losses: float32 [64, 4096], P('pop', 'shard')
- scores: float32 [64], P('pop')
- weight_step: bfloat16 [4096, 1024], P('shard')
Inputs may be any that keep to these rules, and one draw needn't show every extreme that they name: Positions t < lengths[m] of member m are live; the lengths of all members sum to 163840, and some member has exactly 4096. `fitness_ranks`: each of 0 to 63 appears once.
All inputs are finite; a program needn't handle non-finite values. No bound on the sum of `lengths` on one device may be relied on, other than what follows from the above.
Results may differ from a plain program's by a relative error of at most 0.0048.
Values may be sent and summed in bfloat16 or wider, within the bound.
A program may use at most 64 MiB of HBM per device.

v0:
```python
import math
import jax
import jax.numpy as jnp
from jax import lax
from jax.sharding import PartitionSpec as P

noise_scale = 0.1
epsilon = 1e-05


def on_device(
    hidden,
    norm_scale_vector,
    w_value,
    model_side_factor,
    value_side_factor,
    target,
    lengths,
    fitness_ranks,
):
    members, span_here, width = hidden.shape
    share, outputs = w_value.shape
    everyone = fitness_ranks.shape[0]
    widened = hidden.astype(jnp.float32)
    inverse = lax.rsqrt(jnp.mean(widened * widened, axis=-1, keepdims=True) + epsilon)
    normalized_input = (widened * inverse * norm_scale_vector).astype(jnp.bfloat16)
    flattened = normalized_input.reshape(members * span_here, width)
    projected = jnp.dot(
        flattened,
        lax.all_gather(w_value, "shard", axis=0, tiled=True),
        preferred_element_type=jnp.float32,
    )
    reduced_output = jnp.einsum(
        "uch,ufh->ucf", normalized_input, model_side_factor, preferred_element_type=jnp.float32
    ).astype(jnp.bfloat16)
    lateral_product = jnp.einsum(
        "nfw,nwx->nfx", reduced_output, value_side_factor, preferred_element_type=jnp.float32
    )
    values = projected.reshape(members, span_here, outputs) + noise_scale * lateral_product
    errors = values - target.astype(jnp.float32)
    squared = jnp.mean(errors * errors, axis=-1)
    first_position = lax.axis_index("shard") * span_here
    position = first_position + lax.broadcasted_iota(jnp.int32, (members, span_here), 1)
    losses = jnp.where(position < lengths[:, None], squared, 0.0)
    totals = lax.psum(jnp.sum(losses, axis=1), "shard")
    scores = totals / lengths.astype(jnp.float32)
    column_start = lax.axis_index("shard") * share
    left_rows = lax.dynamic_slice_in_dim(model_side_factor, column_start, share, 2)
    step_factor = math.sqrt(width) / (noise_scale * everyone)
    own_ranks = lax.dynamic_slice_in_dim(fitness_ranks, lax.axis_index("pop") * members, members, 0)
    own_fitness = own_ranks.astype(jnp.float32) / (everyone - 1) - 0.5
    scaled_left = (left_rows.astype(jnp.float32) * own_fitness[:, None, None]).astype(jnp.bfloat16)
    pack = jnp.concatenate([scaled_left, value_side_factor], axis=2)
    pack = pack.reshape(pack.shape[0] * pack.shape[1], pack.shape[2])
    everything = lax.all_gather(pack, "pop", axis=0, tiled=True)
    summed_step = lax.dot_general(
        everything[:, :share],
        everything[:, share:],
        (((0,), (0,)), ((), ())),
        preferred_element_type=jnp.float32,
    )
    weight_step = (summed_step * step_factor).astype(jnp.bfloat16)
    return (losses, scores, weight_step)


def solution(mesh):
    placed = (
        P("pop", "shard", None),
        P(),
        P("shard", None),
        P("pop", None, None),
        P("pop", None, None),
        P("pop", "shard", None),
        P("pop"),
        P(),
    )
    return jax.shard_map(
        on_device,
        mesh=mesh,
        in_specs=placed,
        out_specs=(P("pop", "shard"), P("pop"), P("shard", None)),
        check_vma=False,
    )
```

profile of v0, /device:TPU:6, one launch (start us, length us, event | category | flops | bytes accessed | tf_op | source)
XLA Modules:
  0.0 162.0 jit_solution(4412377680226571423)
XLA Ops:
  7.2 0.0 copy-start.4
  7.2 0.0 all-gather.2.cloned.1.call-start
  7.2 0.7 all-gather.2.cloned.1.call-update
  7.9 0.7 multiply_add_fusion
  8.7 0.8 multiply_convert_fusion.1
  9.4 0.7 pad_maximum_fusion
  10.2 5.1 %fusion = f32[2,512]{1,0:T(2,128)S(1)} fusion(bf16[2,512,4096]{2,1,0:T(8,128)(2,1)} %param.8), kind=kLoop, calls=%fused_computation.2 | loop fusion | flops 12581888 | bytes 8392704 | tf_op jit(solution)/shard_map/reduce_sum | solution.py:25
  15.3 41.3 %all_gather.7 = bf16[256,1536]{1,0:T(8,128)(2,1)S(1)} all-gather(bf16[8,1536]{1,0:T(8,128)(2,1)S(1)} %reshape.24), channel_id=1, replica_groups=mesh['pop'=32,'shard'=8] {'pop'}, dimensions={0}, use_global_device_ids=true | all-gather | bytes 811008 | tf_op jit(solution)/shard_map/all_gather | solution.py:55
  56.6 1.4 multiply_convert_fusion
  58.0 0.0 copy-start
  58.0 0.0 copy-start.1
  58.0 0.0 copy-start.3
  58.0 51.7 %all-gather.2.cloned.1.call-done = bf16[4096,1024]{1,0:T(8,128)(2,1)} async-done(((bf16[512,1024]{1,0:T(8,128)(2,1)}), bf16[4096,1024]{1,0:T(8,128)(2,1)}) %all-gather.2.cloned.1.call-update) | async-done | bytes 8388624 | tf_op jit(solution)/shard_map/all_gather | solution.py:30
  109.7 0.0 copy-done.4
  109.7 15.1 %fusion.3 = f32[2,512,1024]{2,1,0:T(8,128)} fusion(bf16[4096,1024]{1,0:T(8,128)(2,1)} %all-gather.2.cloned.1.call-done, bf16[2,512,4096]{2,1,0:T(8,128)(2,1)} %param.8, f32[4096]{0:T(1024)S(1)} %copy-done.4, f32[2,512]{1,0:T(2,128)S(1)} %add_rsqrt_fusion), kind=kOutput, calls=%fused_computation.5 | convolution fusion | flops 8606711808 | bytes 20992000 | tf_op jit(solution)/shard_map/dot_general | solution.py:28
  124.8 0.0 copy-done
  124.8 0.0 copy-done.1
  124.8 0.0 copy-done.3
  124.8 0.0 copy-start.2
  124.8 8.0 %multiply_reduce_fusion = f32[2,512]{1,0:T(2,128)S(1)} fusion(bf16[2,512,1024]{2,1,0:T(8,128)(2,1)S(1)} %copy-done.3, f32[2,512,1024]{2,1,0:T(8,128)} %fusion.3, bf16[2,4,1024]{2,1,0:T(4,128)(2,1)S(1)} %copy-done, bf16[2,4,4096]{2,1,0:T(4,128)(2,1)S(1)} %copy-done.1, bf16[2,512,4096]{2,1,0:T(8,128)(2,1)} %param.8, f32[4096]{0:T(1024)S(1)} %copy-done.4, ...), kind=kOutput, calls=%fused_computation.8 | convolution fusion | flops 65014784 | bytes 14786560 | tf_op jit(solution)/shard_map/nfw,nwx->nfx/dot_general | solution.py:36
  132.9 0.0 copy-done.2
  132.9 0.8 fusion.15
  133.6 21.0 %psum.7 = f32[2]{0:T(128)S(1)} all-reduce(f32[2]{0:T(128)S(1)} %get-tuple-element.3), channel_id=1, replica_groups=mesh['pop'=32,'shard'=8] {'shard'}, use_global_device_ids=true, to_apply=%region_3.4 | all-reduce | flops 2 | bytes 16 | tf_op jit(solution)/shard_map/psum | solution.py:45
  154.6 0.5 convert_divide_fusion
  (3 shorter events, 0.0 us)
Async XLA Ops:
  7.2 102.6 %copy-start.4 = (f32[4096]{0:T(1024)S(1)}, f32[4096]{0:T(1024)}, u32[]{:S(2)}) copy-start(f32[4096]{0:T(1024)} %param.9) | copy-start | bytes 49156
  7.2 102.6 %all-gather.2.cloned.1.call-start = ((), (), s32[]{:S(2)}) async-start(), calls=%async_computation | async-start | bytes 9437184 | tf_op jit(solution)/shard_map/all_gather | solution.py:30
  58.0 66.8 %copy-start = (bf16[2,4,1024]{2,1,0:T(4,128)(2,1)S(1)}, bf16[2,4,1024]{2,1,0:T(4,128)(2,1)}, u32[]{:S(2)}) copy-start(bf16[2,4,1024]{2,1,0:T(4,128)(2,1)} %param.12) | copy-start | bytes 49156
  58.0 66.8 %copy-start.1 = (bf16[2,4,4096]{2,1,0:T(4,128)(2,1)S(1)}, bf16[2,4,4096]{2,1,0:T(4,128)(2,1)}, u32[]{:S(2)}) copy-start(bf16[2,4,4096]{2,1,0:T(4,128)(2,1)} %param.11) | copy-start | bytes 196612
  58.0 66.8 %copy-start.3 = (bf16[2,512,1024]{2,1,0:T(8,128)(2,1)S(1)}, bf16[2,512,1024]{2,1,0:T(8,128)(2,1)}, u32[]{:S(2)}) copy-start(bf16[2,512,1024]{2,1,0:T(8,128)(2,1)} %param.13) | copy-start | bytes 6291460
  124.8 8.0 %copy-start.2 = (s32[2]{0:T(128)S(1)}, s32[2]{0:T(128)}, u32[]{:S(2)}) copy-start(s32[2]{0:T(128)} %param.14) | copy-start | bytes 28
Sparse Core Ops, SparseCore 0:
  9.8 99.8 all-gather.1
where the time goes:
time: 162 us
  blocking collectives  62.3 us (38%)
  waiting for transfers between devices  52.4 us (32%)
  matrix products  24.5 us (15%)
  between operations  14.1 us (9%)
  other arithmetic  8.63 us (5%)
    all_gather x1, waiting for transfers between devices, on_device(): lax.all_gather(w_value, 'shard', axis=0, tiled=True)  51.7 us
    all_gather x1, blocking collectives, on_device(): everything = lax.all_gather(pack, 'pop', axis=0, tiled=True)  41.3 us
    psum x1, blocking collectives, on_device(): totals = lax.psum(jnp.sum(losses, axis=1), 'shard')  21 us
    dot_general x1, matrix products, on_device(): jnp.dot(flattened, lax.all_gather(w_value, 'shard', axis=0, tiled=True),...  15.1 us
    dot_general x1, matrix products, on_device(): jnp.einsum('nfw,nwx->nfx', reduced_output, value_side_factor, preferred_e...  8 us
    reduce_sum x1, other arithmetic, on_device(): jnp.mean(widened * widened, axis=-1, keepdims=True) + epsilon  5.08 us
  transfers between devices with their start and end apart: 1, of which 1 were waited for; matrix products, arithmetic and copies ran while one was open for 5% of the time, Pallas kernels for 0%

commit v1 on v0

--- a/solution.py
+++ b/solution.py
@@ -52,7 +52,9 @@
     scaled_left = (left_rows.astype(jnp.float32) * own_fitness[:, None, None]).astype(jnp.bfloat16)
     pack = jnp.concatenate([scaled_left, value_side_factor], axis=2)
     pack = pack.reshape(pack.shape[0] * pack.shape[1], pack.shape[2])
-    everything = lax.all_gather(pack, "pop", axis=0, tiled=True)
+    everything = jnp.concatenate(
+        lax.all_to_all(jnp.stack([pack] * lax.axis_size("pop")), "pop", 0, 0), axis=0
+    )
     summed_step = lax.dot_general(
         everything[:, :share],
         everything[:, share:],

time: 162 us -> 172 us (1.062)
  blocking collectives: 62.3 us -> 16.6 us
  waiting for transfers between devices: 52.4 us -> 94.5 us
  starting transfers between devices: 0.04 us -> 11.6 us
    all_gather x1 -> x0, blocking collectives: 41.3 us -> none  [on_device(): everything = lax.all_gather(pack, 'pop', axis=0, tiled=True)]
    all_to_all x0 -> x1, waiting for transfers between devices: none -> 25.7 us  [on_device(): lax.all_to_all(jnp.stack([pack] * lax.axis_size('pop')), 'pop', 0, 0)]
    all_gather x1, waiting for transfers between devices: 51.7 us -> 68.1 us  [on_device(): lax.all_gather(w_value, 'shard', axis=0, tiled=True)]
    all_to_all x0 -> x1, starting transfers between devices: none -> 11.6 us  [on_device(): lax.all_to_all(jnp.stack([pack] * lax.axis_size('pop')), 'pop', 0, 0)]
    psum x1, blocking collectives: 21 us -> 16.6 us  [on_device(): totals = lax.psum(jnp.sum(losses, axis=1), 'shard')]
  transfers between devices with their start and end apart: 1 -> 2, of which waited for: 1 -> 2; matrix products, arithmetic and copies ran while one was open for 5% -> 6% of each run, Pallas kernels for 0% -> 0%
where the time goes in v1:
time: 172 us; the launch traced here: 171 us
  waiting for transfers between devices  94.5 us (55%)
  matrix products  24.5 us (14%)
  blocking collectives  16.6 us (10%)
  between operations  14.1 us (8%)
  starting transfers between devices  11.6 us (7%)
  other arithmetic  8.98 us (5%)
    all_gather x1, waiting for transfers between devices, on_device(): lax.all_gather(w_value, 'shard', axis=0, tiled=True)  68.1 us
    all_to_all x1, waiting for transfers between devices, on_device(): lax.all_to_all(jnp.stack([pack] * lax.axis_size('pop')), 'pop', 0, 0)  25.7 us
    psum x1, blocking collectives, on_device(): totals = lax.psum(jnp.sum(losses, axis=1), 'shard')  16.6 us
    dot_general x1, matrix products, on_device(): jnp.dot(flattened, lax.all_gather(w_value, 'shard', axis=0, tiled=True),...  15.1 us
    all_to_all x1, starting transfers between devices, on_device(): lax.all_to_all(jnp.stack([pack] * lax.axis_size('pop')), 'pop', 0, 0)  11.6 us
    dot_general x1, matrix products, on_device(): jnp.einsum('nfw,nwx->nfx', reduced_output, value_side_factor, preferred_e...  7.98 us
    reduce_sum x1, other arithmetic, on_device(): jnp.mean(widened * widened, axis=-1, keepdims=True) + epsilon  5.43 us
  transfers between devices with their start and end apart: 2, of which 2 were waited for; matrix products, arithmetic and copies ran while one was open for 6% of the time, Pallas kernels for 0%

profile of v1, /device:TPU:6, one launch (start us, length us, event | category | flops | bytes accessed | tf_op | source)
XLA Modules:
  0.0 171.2 jit_solution(2653734034494230441)
XLA Ops:
  7.2 0.0 copy-start.4
  7.2 0.0 all-gather.2.cloned.1.call-start
  7.2 0.7 all-gather.2.cloned.1.call-update
  7.9 0.7 multiply_add_fusion
  8.7 0.8 multiply_convert_fusion.1
  9.4 0.7 pad_maximum_fusion
  10.2 0.9 stack.3
  11.1 11.6 %all-to-all-start = ((bf16[32,8,1536]{2,1,0:T(8,128)(2,1)}), bf16[32,8,1536]{2,1,0:T(8,128)(2,1)S(1)}, u32[]{:S(2)}, u32[]{:S(2)}) async-start(bf16[32,8,1536]{2,1,0:T(8,128)(2,1)} %stack.3), calls=%async_computation | async-start | bytes 1572864 | tf_op jit(solution)/shard_map/all_to_all | solution.py:56
  22.7 5.4 %fusion = f32[2,512]{1,0:T(2,128)S(1)} fusion(bf16[2,512,4096]{2,1,0:T(8,128)(2,1)} %param.8), kind=kLoop, calls=%fused_computation.2 | loop fusion | flops 12581888 | bytes 8392704 | tf_op jit(solution)/shard_map/reduce_sum | solution.py:25
  28.1 25.7 %all-to-all-done = bf16[32,8,1536]{2,1,0:T(8,128)(2,1)S(1)} async-done(((bf16[32,8,1536]{2,1,0:T(8,128)(2,1)}), bf16[32,8,1536]{2,1,0:T(8,128)(2,1)S(1)}, u32[]{:S(2)}, u32[]{:S(2)}) %all-to-all-start) | async-done | bytes 786464 | tf_op jit(solution)/shard_map/all_to_all | solution.py:56
  53.8 1.4 multiply_convert_fusion
  55.3 0.0 copy-start
  55.3 0.0 copy-start.1
  55.3 0.0 copy-start.3
  55.3 68.1 %all-gather.2.cloned.1.call-done = bf16[4096,1024]{1,0:T(8,128)(2,1)} async-done(((bf16[512,1024]{1,0:T(8,128)(2,1)}), bf16[4096,1024]{1,0:T(8,128)(2,1)}) %all-gather.2.cloned.1.call-update) | async-done | bytes 8388624 | tf_op jit(solution)/shard_map/all_gather | solution.py:30
  123.4 0.0 copy-done.4
  123.4 15.1 %fusion.3 = f32[2,512,1024]{2,1,0:T(8,128)} fusion(bf16[4096,1024]{1,0:T(8,128)(2,1)} %all-gather.2.cloned.1.call-done, bf16[2,512,4096]{2,1,0:T(8,128)(2,1)} %param.8, f32[4096]{0:T(1024)S(1)} %copy-done.4, f32[2,512]{1,0:T(2,128)S(1)} %add_rsqrt_fusion), kind=kOutput, calls=%fused_computation.5 | convolution fusion | flops 8606711808 | bytes 20992000 | tf_op jit(solution)/shard_map/dot_general | solution.py:28
  138.5 0.0 copy-done
  138.5 0.0 copy-done.1
  138.5 0.0 copy-done.3
  138.5 0.0 copy-start.2
  138.5 8.0 %multiply_reduce_fusion = f32[2,512]{1,0:T(2,128)S(1)} fusion(bf16[2,512,1024]{2,1,0:T(8,128)(2,1)S(1)} %copy-done.3, f32[2,512,1024]{2,1,0:T(8,128)} %fusion.3, bf16[2,4,1024]{2,1,0:T(4,128)(2,1)S(1)} %copy-done, bf16[2,4,4096]{2,1,0:T(4,128)(2,1)S(1)} %copy-done.1, bf16[2,512,4096]{2,1,0:T(8,128)(2,1)} %param.8, f32[4096]{0:T(1024)S(1)} %copy-done.4, ...), kind=kOutput, calls=%fused_computation.8 | convolution fusion | flops 65014784 | bytes 14786560 | tf_op jit(solution)/shard_map/nfw,nwx->nfx/dot_general | solution.py:36
  146.5 0.0 copy-done.2
  146.5 0.8 fusion.15
  147.2 16.6 %psum.7 = f32[2]{0:T(128)S(1)} all-reduce(f32[2]{0:T(128)S(1)} %get-tuple-element.3), channel_id=1, replica_groups=mesh['pop'=32,'shard'=8] {'shard'}, use_global_device_ids=true, to_apply=%region_3.4 | all-reduce | flops 2 | bytes 16 | tf_op jit(solution)/shard_map/psum | solution.py:45
  163.8 0.5 convert_divide_fusion
  (3 shorter events, 0.0 us)
Async XLA Ops:
  7.2 116.2 %copy-start.4 = (f32[4096]{0:T(1024)S(1)}, f32[4096]{0:T(1024)}, u32[]{:S(2)}) copy-start(f32[4096]{0:T(1024)} %param.9) | copy-start | bytes 49156
  7.2 116.2 %all-gather.2.cloned.1.call-start = ((), (), s32[]{:S(2)}) async-start(), calls=%async_computation.1 | async-start | bytes 9437184 | tf_op jit(solution)/shard_map/all_gather | solution.py:30
  11.1 42.7 %all-to-all-start = ((bf16[32,8,1536]{2,1,0:T(8,128)(2,1)}), bf16[32,8,1536]{2,1,0:T(8,128)(2,1)S(1)}, u32[]{:S(2)}, u32[]{:S(2)}) async-start(bf16[32,8,1536]{2,1,0:T(8,128)(2,1)} %stack.3), calls=%async_computation | async-start | bytes 1572864 | tf_op jit(solution)/shard_map/all_to_all | solution.py:56
  55.3 83.2 %copy-start = (bf16[2,4,1024]{2,1,0:T(4,128)(2,1)S(1)}, bf16[2,4,1024]{2,1,0:T(4,128)(2,1)}, u32[]{:S(2)}) copy-start(bf16[2,4,1024]{2,1,0:T(4,128)(2,1)} %param.12) | copy-start | bytes 49156
  55.3 83.2 %copy-start.1 = (bf16[2,4,4096]{2,1,0:T(4,128)(2,1)S(1)}, bf16[2,4,4096]{2,1,0:T(4,128)(2,1)}, u32[]{:S(2)}) copy-start(bf16[2,4,4096]{2,1,0:T(4,128)(2,1)} %param.11) | copy-start | bytes 196612
  55.3 83.2 %copy-start.3 = (bf16[2,512,1024]{2,1,0:T(8,128)(2,1)S(1)}, bf16[2,512,1024]{2,1,0:T(8,128)(2,1)}, u32[]{:S(2)}) copy-start(bf16[2,512,1024]{2,1,0:T(8,128)(2,1)} %param.13) | copy-start | bytes 6291460
  138.5 8.0 %copy-start.2 = (s32[2]{0:T(128)S(1)}, s32[2]{0:T(128)}, u32[]{:S(2)}) copy-start(s32[2]{0:T(128)} %param.14) | copy-start | bytes 28
Sparse Core Ops, SparseCore 0:
  9.8 113.5 all-gather.1
